TPU v7x, 128 devices: a whole 4x4x4 slice. The times are simulated.
128 devices in a mesh: row: 8 (over x, core), col: 16 (over z, y).
Axes of the slice: x: 4, y: 4, z: 4, core: 2. Of those that a mesh axis runs over, the one named last changes fastest.
Arguments:
- model_init: float32 [2, 2, 16, 16384], P(None, None, None, 'col'), may hold values from -2 to 2
- observed: float32 [2, 2, 16, 32768], P(None, None, None, ('row', 'col')), may hold values from -6 to 6
- left_bases: bfloat16 [128, 64, 2, 96, 2, 256], P(('row', 'col')), may hold values from -0.078125 to 0.078125
- right_bases: bfloat16 [128, 64, 2, 96, 2, 256], P('row', 'col'), may hold values from -0.078125 to 0.078125
- tile_ranks: int32 [128, 64, 2], P('row', 'col'), may hold values from 8 to 96
- gate_start: int32 [16, 32768], P(None, ('row', 'col')), may hold values from 0 to 31
- gate_stop: int32 [16, 32768], P(None, ('row', 'col')), may hold values from 32 to 64
Outputs:
- model_final: float32 [2, 2, 16, 16384], P(None, None, None, 'col')
- residual_final: float32 [2, 2, 16, 32768], P(None, None, None, ('row', 'col'))
All inputs are finite; a program needn't handle non-finite values.
Results may differ from a plain program's by a relative error of at most 0.009.
Values may be sent and summed in bfloat16 or wider, within the bound.
No kernel may reach another device: no remote copies, remote signals or barrier semaphores. Data moves between devices by JAX's collectives and lax.ppermute only.
A program may use at most 128 MiB of HBM per device.

v0:
```python
import math
import jax
import jax.numpy as jnp
from jax import lax
from jax.sharding import PartitionSpec as P

NV = 16
TILE = 256
RMAX = 96
F = 2
NT = 64
ITERS = 2
step_length = 0.8


def time_table(samples):
    sample_times = jnp.arange(samples, dtype=jnp.float32)[:, None]
    freq_bins = (3.0 + 5.0 * jnp.arange(F, dtype=jnp.float32))[None, :]
    phases = 2.0 * math.pi * sample_times * freq_bins / samples
    return jnp.concatenate([jnp.cos(phases), -jnp.sin(phases)], axis=1)


def apply_gate(field, gate_start, gate_stop):
    transform = time_table(NT)
    flattened = field.reshape(2 * F, -1)
    signal = jnp.dot(transform, flattened, precision=lax.Precision.HIGHEST)
    sample_index = jnp.arange(NT, dtype=jnp.int32)[:, None, None]
    window = ((sample_index >= gate_start[None]) & (sample_index < gate_stop[None])).astype(
        jnp.float32
    )
    windowed = signal * window.reshape(NT, -1)
    returned = jnp.dot(transform.T, windowed, precision=lax.Precision.HIGHEST) * (2.0 / NT)
    return returned.reshape(field.shape)


def pair_rows(field):
    real_part, imag_part = (field[0], field[1])
    upper_pair = jnp.stack([real_part, imag_part], axis=3)
    lower_pair = jnp.stack([imag_part, -real_part], axis=3)
    joined = jnp.stack([upper_pair, lower_pair], axis=1)
    return jnp.transpose(joined, (3, 0, 1, 2, 4, 5))


def combine(stacked):
    real_part = stacked[:, :, 0, :, 0] - stacked[:, :, 1, :, 1]
    imag_part = stacked[:, :, 0, :, 1] + stacked[:, :, 1, :, 0]
    joined = jnp.stack([real_part, imag_part], axis=0)
    joined = jnp.transpose(joined, (0, 2, 3, 1, 4))
    return joined.reshape(joined.shape[0], joined.shape[1], joined.shape[2], -1)


def forward(low_model, left_bases, right_bases, rank_keep):
    blocks = low_model.shape[3] // TILE
    paired = pair_rows(low_model.reshape(2, F, NV, blocks, TILE))
    coefficients = jnp.einsum(
        "jfavcs,ijfkcs->ijfavk", paired, right_bases, preferred_element_type=jnp.float32
    )
    coefficients = (coefficients * rank_keep[:, :, :, None, None, :]).astype(jnp.bfloat16)
    sendable = coefficients.reshape(coefficients.shape[0], coefficients.shape[1], F, 2, NV * RMAX)
    received = lax.all_to_all(sendable, "col", split_axis=0, concat_axis=1, tiled=True)
    received = received.reshape(received.shape[0], received.shape[1], F, 2, NV, RMAX)
    modeled = jnp.einsum(
        "ijfavk,ijfkcn->ifavcn", received, left_bases, preferred_element_type=jnp.float32
    )
    return combine(modeled)


def adjoint(residual, left_bases, right_bases, rank_keep):
    blocks = residual.shape[3] // TILE
    paired = pair_rows(residual.astype(jnp.bfloat16).reshape(2, F, NV, blocks, TILE))
    coefficients = jnp.einsum(
        "ifavcn,ijfkcn->ijfavk", paired, left_bases, preferred_element_type=jnp.float32
    )
    coefficients = coefficients.astype(jnp.bfloat16)
    sendable = coefficients.reshape(blocks, coefficients.shape[1], F, 2, NV * RMAX)
    received = lax.all_to_all(sendable, "col", split_axis=1, concat_axis=0, tiled=True)
    received = received.reshape(received.shape[0], received.shape[1], F, 2, NV, RMAX)
    received = received * rank_keep[:, :, :, None, None, :].astype(jnp.bfloat16)
    column_terms = jnp.einsum(
        "ijfavk,ijfkcs->jfavcs", received, right_bases, preferred_element_type=jnp.float32
    )
    return combine(column_terms)


def shards(model_init, observed, left_bases, right_bases, tile_ranks, gate_start, gate_stop):
    rank_index = jnp.arange(RMAX, dtype=jnp.int32)
    rank_keep = (rank_index < tile_ranks[..., None]).astype(jnp.float32)
    estimate = model_init
    low_model = model_init.astype(jnp.bfloat16)
    for iteration in range(ITERS):
        predicted = forward(low_model, left_bases, right_bases, rank_keep)
        residual = apply_gate(predicted - observed, gate_start, gate_stop)
        grad_local = adjoint(residual, left_bases, right_bases, rank_keep)
        gradient = lax.psum(grad_local.astype(jnp.bfloat16), "row").astype(jnp.float32)
        estimate = estimate - step_length * gradient
        low_model = estimate.astype(jnp.bfloat16)
    predicted = forward(low_model, left_bases, right_bases, rank_keep)
    residual = apply_gate(predicted - observed, gate_start, gate_stop)
    return (estimate, residual)


def solution(mesh):
    placed = (
        P(None, None, None, "col"),
        P(None, None, None, ("row", "col")),
        P(("row", "col"), None, None, None, None, None),
        P("row", "col", None, None, None, None),
        P("row", "col", None),
        P(None, ("row", "col")),
        P(None, ("row", "col")),
    )
    return jax.shard_map(
        shards,
        mesh=mesh,
        in_specs=placed,
        out_specs=(P(None, None, None, "col"), P(None, None, None, ("row", "col"))),
        check_vma=False,
    )
```

profile of v0, /device:TPU:6, one launch (start us, length us, event | category | flops | bytes accessed | tf_op | source)
XLA Modules:
  0.0 333.3 jit_solution(16784469923808730853)
XLA Ops:
  7.2 0.8 fusion.96
  8.0 1.0 convert_element_type.93
  9.1 9.1 %fusion.24 = bf16[16,4,2,2,16,96]{5,4,0,3,2,1:T(8,128)(2,1)S(1)} fusion(bf16[16,4,2,96,2,256,1]{5,4,3,2,1,0,6:T(2,128)(2,1)} %bitcast.384, f32[16,4,2,96]{3,0,2,1:T(8,128)S(1)} %get-tuple-element.31, bf16[2,1,16,4,2,256]{5,2,4,1,0,3:T(8,128)(2,1)S(1)} %get-tuple-element.19, bf16[2,1,16,4,2,256]{5,2,4,1,0,3:T(8,128)(2,1)S(1)} %get-tuple-element.18), kind=kOutput, calls=%fused_computation.33 | convolution fusion | flops 403963904 | bytes 13680640 | tf_op jit(solution)/shard_map/jfavcs,ijfkcs->ijfavk/dot_general | solution.py:55
  18.2 1.2 reshape.437
  19.4 1.7 copy.96
  21.1 8.4 %all-to-all-start = ((bf16[16,4,2,2,1536]{4,3,2,1,0:T(2,128)(2,1)}), bf16[16,4,2,2,1536]{4,3,2,1,0:T(2,128)(2,1)S(1)}, u32[]{:S(2)}, u32[]{:S(2)}) async-start(bf16[16,4,2,2,1536]{4,3,2,1,0:T(2,128)(2,1)} %copy.96), calls=%async_computation | async-start | bytes 1572864 | tf_op jit(solution)/shard_map/all_to_all | solution.py:60
  29.7 14.3 %all-to-all-done = bf16[16,4,2,2,1536]{4,3,2,1,0:T(2,128)(2,1)S(1)} async-done(((bf16[16,4,2,2,1536]{4,3,2,1,0:T(2,128)(2,1)}), bf16[16,4,2,2,1536]{4,3,2,1,0:T(2,128)(2,1)S(1)}, u32[]{:S(2)}, u32[]{:S(2)}) %all-to-all-start) | async-done | bytes 786464 | tf_op jit(solution)/shard_map/all_to_all | solution.py:60
  44.3 0.9 reshape.457
  45.2 6.9 %fusion.47 = f32[1,2,2,16,2,256]{5,3,4,2,1,0:T(8,128)S(1)} fusion(bf16[64,2,96,2,256,1]{4,3,2,1,0,5:T(2,128)(2,1)} %bitcast.353, bf16[64,2,2,16,96,1]{4,3,0,2,1,5:T(8,128)(2,1)S(1)} %reshape.457), kind=kOutput, calls=%fused_computation.40 | convolution fusion | flops 402653184 | bytes 13500416 | tf_op jit(solution)/shard_map/ijfavk,ijfkcn->ifavcn/dot_general | solution.py:62
  52.2 1.2 convolution_select_fusion.2
  53.4 0.6 fusion.20
  54.1 7.6 %fusion.35 = bf16[1,64,2,2,16,96]{5,4,1,3,2,0:T(8,128)(2,1)S(1)} fusion(bf16[64,2,96,2,256,1]{4,3,2,1,0,5:T(2,128)(2,1)} %bitcast.354, bf16[2,1,16,1,2,256]{5,2,4,1,0,3:T(8,128)(2,1)S(1)} %get-tuple-element.29, bf16[2,1,16,1,2,256]{5,2,4,1,0,3:T(8,128)(2,1)S(1)} %get-tuple-element.28), kind=kOutput, calls=%fused_computation.36 | convolution fusion | flops 403177472 | bytes 13434880 | tf_op jit(solution)/shard_map/ifavcn,ijfkcn->ijfavk/dot_general | solution.py:71
  61.8 1.2 reshape.442
  63.0 1.7 copy.106
  64.7 3.6 %all-to-all-start.1 = ((bf16[1,64,2,2,1536]{4,3,2,0,1:T(2,128)(2,1)}), bf16[1,64,2,2,1536]{4,3,2,0,1:T(2,128)(2,1)S(1)}, u32[]{:S(2)}, u32[]{:S(2)}) async-start(bf16[1,64,2,2,1536]{4,3,2,0,1:T(2,128)(2,1)} %copy.106), calls=%async_computation.1 | async-start | bytes 1572864 | tf_op jit(solution)/shard_map/all_to_all | solution.py:76
  68.3 0.6 all-reduce.3.cloned.1.call-start
  69.0 12.5 %all-to-all-done.1 = bf16[1,64,2,2,1536]{4,3,2,0,1:T(2,128)(2,1)S(1)} async-done(((bf16[1,64,2,2,1536]{4,3,2,0,1:T(2,128)(2,1)}), bf16[1,64,2,2,1536]{4,3,2,0,1:T(2,128)(2,1)S(1)}, u32[]{:S(2)}, u32[]{:S(2)}) %all-to-all-start.1) | async-done | bytes 786464 | tf_op jit(solution)/shard_map/all_to_all | solution.py:76
  81.6 0.9 reshape.443
  82.5 6.9 %fusion.41 = f32[4,2,2,16,2,256]{5,3,4,2,1,0:T(8,128)S(1)} fusion(bf16[16,4,2,96,2,256,1]{5,4,3,2,1,0,6:T(2,128)(2,1)} %bitcast.385, bf16[16,4,2,2,16,96]{5,4,1,0,3,2:T(8,128)(2,1)S(1)} %reshape.443, bf16[16,4,2,96]{3,1,0,2:T(4,128)(2,1)S(1)} %copy.108), kind=kOutput, calls=%fused_computation.38 | convolution fusion | flops 403046400 | bytes 13918208 | tf_op jit(solution)/shard_map/ijfavk,ijfkcs->jfavcs/dot_general | solution.py:79
  89.5 0.7 copy.210
  90.2 55.2 %all-reduce.3.cloned.1.call-done = bf16[2,2,16,1024]{3,2,1,0:T(8,128)(2,1)} async-done(((bf16[2,2,16,1024]{3,2,1,0:T(8,128)(2,1)}), bf16[2,2,16,1024]{3,2,1,0:T(8,128)(2,1)}) %all-reduce.3.cloned.1.call-update) | async-done | bytes 131088 | tf_op jit(solution)/shard_map/psum | solution.py:94
  145.4 0.9 fusion.68
  146.6 9.1 %fusion.23 = bf16[16,4,2,2,16,96]{5,4,0,3,2,1:T(8,128)(2,1)S(1)} fusion(bf16[16,4,2,96,2,256,1]{5,4,3,2,1,0,6:T(2,128)(2,1)} %bitcast.386, f32[16,4,2,96]{3,0,2,1:T(8,128)S(1)} %get-tuple-element.31, bf16[2,1,16,4,2,256]{5,2,4,1,0,3:T(8,128)(2,1)S(1)} %get-tuple-element.15, bf16[2,1,16,4,2,256]{5,2,4,1,0,3:T(8,128)(2,1)S(1)} %get-tuple-element.14), kind=kOutput, calls=%fused_computation.31 | convolution fusion | flops 403963904 | bytes 13680640 | tf_op jit(solution)/shard_map/jfavcs,ijfkcs->ijfavk/dot_general | solution.py:55
  155.7 1.2 reshape.444
  156.9 0.8 copy.119
  157.7 22.1 %all_to_all.20 = bf16[16,4,2,2,1536]{4,3,2,1,0:T(2,128)(2,1)S(1)} all-to-all(bf16[16,4,2,2,1536]{4,3,2,1,0:T(2,128)(2,1)S(1)} %copy.119), channel_id=1, replica_groups=mesh['row'=8,'col'=16] {'col'}, dimensions={0} | all-to-all | bytes 1572864 | tf_op jit(solution)/shard_map/all_to_all | solution.py:60
  180.1 0.9 reshape.469
  181.0 6.9 %fusion.50 = f32[1,2,2,16,2,256]{5,3,4,2,1,0:T(8,128)S(1)} fusion(bf16[64,2,96,2,256,1]{4,3,2,1,0,5:T(2,128)(2,1)} %bitcast.355, bf16[64,2,2,16,96,1]{4,3,0,2,1,5:T(8,128)(2,1)S(1)} %reshape.469), kind=kOutput, calls=%fused_computation.41 | convolution fusion | flops 402653184 | bytes 13500416 | tf_op jit(solution)/shard_map/ijfavk,ijfkcn->ifavcn/dot_general | solution.py:62
  188.0 1.2 convolution_select_fusion.1
  189.2 0.6 fusion.21
  189.9 7.6 %fusion.38 = bf16[1,64,2,2,16,96]{5,4,1,3,2,0:T(8,128)(2,1)S(1)} fusion(bf16[64,2,96,2,256,1]{4,3,2,1,0,5:T(2,128)(2,1)} %bitcast.356, bf16[2,1,16,1,2,256]{5,2,4,1,0,3:T(8,128)(2,1)S(1)} %get-tuple-element.27, bf16[2,1,16,1,2,256]{5,2,4,1,0,3:T(8,128)(2,1)S(1)} %get-tuple-element.26), kind=kOutput, calls=%fused_computation.37 | convolution fusion | flops 403177472 | bytes 13434880 | tf_op jit(solution)/shard_map/ifavcn,ijfkcn->ijfavk/dot_general | solution.py:71
  197.5 1.2 reshape.448
  198.7 0.8 copy.129
  199.6 17.2 %all_to_all.21 = bf16[1,64,2,2,1536]{4,3,2,0,1:T(2,128)(2,1)S(1)} all-to-all(bf16[1,64,2,2,1536]{4,3,2,0,1:T(2,128)(2,1)S(1)} %copy.129), channel_id=1, replica_groups=mesh['row'=8,'col'=16] {'col'}, dimensions={1} | all-to-all | bytes 1572864 | tf_op jit(solution)/shard_map/all_to_all | solution.py:76
  216.9 0.9 reshape.449
  217.8 6.9 %fusion.44 = f32[4,2,2,16,2,256]{5,3,4,2,1,0:T(8,128)S(1)} fusion(bf16[16,4,2,96,2,256,1]{5,4,3,2,1,0,6:T(2,128)(2,1)} %bitcast.387, bf16[16,4,2,2,16,96]{5,4,1,0,3,2:T(8,128)(2,1)S(1)} %reshape.449, bf16[16,4,2,96]{3,1,0,2:T(4,128)(2,1)S(1)} %copy.108), kind=kOutput, calls=%fused_computation.39 | convolution fusion | flops 403046400 | bytes 13918208 | tf_op jit(solution)/shard_map/ijfavk,ijfkcs->jfavcs/dot_general | solution.py:79
  224.8 0.7 copy.211
  225.5 54.9 %all-reduce.5.cloned.1.call-done = bf16[2,2,16,1024]{3,2,1,0:T(8,128)(2,1)} async-done(((bf16[2,2,16,1024]{3,2,1,0:T(8,128)(2,1)}), bf16[2,2,16,1024]{3,2,1,0:T(8,128)(2,1)}) %all-reduce.5.cloned.1.call-update) | async-done | bytes 131088 | tf_op jit(solution)/shard_map/psum | solution.py:94
  280.3 1.7 fusion.105
  282.2 9.1 %fusion.22 = bf16[16,4,2,2,16,96]{5,4,0,3,2,1:T(8,128)(2,1)S(1)} fusion(bf16[16,4,2,96,2,256,1]{5,4,3,2,1,0,6:T(2,128)(2,1)} %bitcast.388, f32[16,4,2,96]{3,0,2,1:T(8,128)S(1)} %get-tuple-element.31, bf16[2,1,16,4,2,256]{5,2,4,1,0,3:T(8,128)(2,1)S(1)} %get-tuple-element.11, bf16[2,1,16,4,2,256]{5,2,4,1,0,3:T(8,128)(2,1)S(1)} %get-tuple-element.10), kind=kOutput, calls=%fused_computation.29 | convolution fusion | flops 403963904 | bytes 13680640 | tf_op jit(solution)/shard_map/jfavcs,ijfkcs->ijfavk/dot_general | solution.py:55
  291.3 1.2 reshape.450
  292.5 0.8 copy.141
  293.3 22.2 %all_to_all.22 = bf16[16,4,2,2,1536]{4,3,2,1,0:T(2,128)(2,1)S(1)} all-to-all(bf16[16,4,2,2,1536]{4,3,2,1,0:T(2,128)(2,1)S(1)} %copy.141), channel_id=1, replica_groups=mesh['row'=8,'col'=16] {'col'}, dimensions={0} | all-to-all | bytes 1572864 | tf_op jit(solution)/shard_map/all_to_all | solution.py:60
  315.8 0.9 reshape.481
  316.7 6.9 %fusion.53 = f32[1,2,2,16,2,256]{5,3,4,2,1,0:T(8,128)S(1)} fusion(bf16[64,2,96,2,256,1]{4,3,2,1,0,5:T(2,128)(2,1)} %bitcast.357, bf16[64,2,2,16,96,1]{4,3,0,2,1,5:T(8,128)(2,1)S(1)} %reshape.481), kind=kOutput, calls=%fused_computation.42 | convolution fusion | flops 402653184 | bytes 13500416 | tf_op jit(solution)/shard_map/ijfavk,ijfkcn->ifavcn/dot_general | solution.py:62
  323.7 1.2 convolution_select_fusion
  324.9 0.6 convolution_multiply_fusion
  325.5 0.6 copy.221
  (69 shorter events, 2.3 us)
Async XLA Ops:
  7.2 22.3 %copy-start.3 = (s32[16,256]{1,0:T(8,128)S(1)}, s32[16,256]{1,0:T(8,128)}, u32[]{:S(2)}) copy-start(s32[16,256]{1,0:T(8,128)} %param.12) | copy-start | bytes 49156
  7.2 22.4 %copy-start.4 = (s32[16,256]{1,0:T(8,128)S(1)}, s32[16,256]{1,0:T(8,128)}, u32[]{:S(2)}) copy-start(s32[16,256]{1,0:T(8,128)} %param.13) | copy-start | bytes 49156
  18.2 33.9 %copy-start.1 = (f32[2,2,16,256]{3,2,1,0:T(8,128)S(1)}, f32[2,2,16,256]{3,2,1,0:T(8,128)}, u32[]{:S(2)}) copy-start(f32[2,2,16,256]{3,2,1,0:T(8,128)} %param.8) | copy-start | bytes 196612
  21.1 22.9 %all-to-all-start = ((bf16[16,4,2,2,1536]{4,3,2,1,0:T(2,128)(2,1)}), bf16[16,4,2,2,1536]{4,3,2,1,0:T(2,128)(2,1)S(1)}, u32[]{:S(2)}, u32[]{:S(2)}) async-start(bf16[16,4,2,2,1536]{4,3,2,1,0:T(2,128)(2,1)} %copy.96), calls=%async_computation | async-start | bytes 1572864 | tf_op jit(solution)/shard_map/all_to_all | solution.py:60
  61.8 83.7 %copy-start = (f32[2,2,16,1024]{3,2,1,0:T(8,128)S(1)}, f32[2,2,16,1024]{3,2,1,0:T(8,128)}, u32[]{:S(2)}) copy-start(f32[2,2,16,1024]{3,2,1,0:T(8,128)} %param.7) | copy-start | bytes 786436
  64.7 16.8 %all-to-all-start.1 = ((bf16[1,64,2,2,1536]{4,3,2,0,1:T(2,128)(2,1)}), bf16[1,64,2,2,1536]{4,3,2,0,1:T(2,128)(2,1)S(1)}, u32[]{:S(2)}, u32[]{:S(2)}) async-start(bf16[1,64,2,2,1536]{4,3,2,0,1:T(2,128)(2,1)} %copy.106), calls=%async_computation.1 | async-start | bytes 1572864 | tf_op jit(solution)/shard_map/all_to_all | solution.py:76
  68.3 77.1 %all-reduce.3.cloned.1.call-start = ((), (), s32[]{:S(2)}) async-start(), calls=%async_computation.5 | async-start | bytes 262144 | tf_op jit(solution)/shard_map/psum | solution.py:94
  90.2 190.2 %all-reduce.5.cloned.1.call-start = ((), (), s32[]{:S(2)}) async-start(), calls=%async_computation.6 | async-start | bytes 262144 | tf_op jit(solution)/shard_map/psum | solution.py:94
  197.5 82.8 %copy-start.2 = (bf16[2,2,16,1024]{3,2,1,0:T(8,128)(2,1)S(1)}, bf16[2,2,16,1024]{3,2,1,0:T(8,128)(2,1)}, u32[]{:S(2)}) copy-start(bf16[2,2,16,1024]{3,2,1,0:T(8,128)(2,1)} %all-reduce.3.cloned.1.call-done) | copy-start | bytes 393220
Sparse Core Ops, SparseCore 0:
  90.3 55.1 all-reduce.2
  225.6 54.6 all-reduce.4
where the time goes:
time: 338 us; the launch traced here: 333 us
  waiting for transfers between devices  137 us (41%)
  matrix products  82.3 us (24%)
  blocking collectives  61.5 us (18%)
  local copies, waits for them, and re-layouts  20.1 us (6%)
  between operations  14.9 us (4%)
  starting transfers between devices  12.7 us (4%)
  other arithmetic  4.85 us (1%)
    psum x2, waiting for transfers between devices, shards(): lax.psum(grad_local.astype(jnp.bfloat16), 'row').astype(jnp.float32)  110 us
    all_to_all x2, blocking collectives, forward(): lax.all_to_all(sendable, 'col', split_axis=0, concat_axis=1, tiled=True)  44.3 us
    dot_general x3, matrix products, forward(): jnp.einsum('jfavcs,ijfkcs->ijfavk', paired, right_bases, preferred_elemen...  27.3 us
    dot_general x3, matrix products, forward(): jnp.einsum('ijfavk,ijfkcn->ifavcn', received, left_bases, preferred_eleme...  20.6 us
    all_to_all x1, blocking collectives, adjoint(): lax.all_to_all(sendable, 'col', split_axis=1, concat_axis=0, tiled=True)  17.2 us
    dot_general x2, matrix products, adjoint(): jnp.einsum('ifavcn,ijfkcn->ijfavk', paired, left_bases, preferred_element...  15.2 us
    all_to_all x1, waiting for transfers between devices, forward(): lax.all_to_all(sendable, 'col', split_axis=0, concat_axis=1, tiled=True)  14.3 us
    dot_general x2, matrix products, adjoint(): jnp.einsum('ijfavk,ijfkcs->jfavcs', received, right_bases, preferred_elem...  13.8 us
  transfers between devices with their start and end apart: 4, of which 4 were waited for; matrix products, arithmetic and copies ran while one was open for 0% of the time, Pallas kernels for 0%

commit v1 on v0

--- a/solution.py
+++ b/solution.py
@@ -11,6 +11,12 @@
 NT = 64
 ITERS = 2
 step_length = 0.8
+
+
+def summed_here(shard, axis):
+    shards = lax.all_gather(shard, axis, axis=0, tiled=False)
+    total = shards.sum(axis=0)
+    return total
 
 
 def time_table(samples):
@@ -91,7 +97,7 @@
         predicted = forward(low_model, left_bases, right_bases, rank_keep)
         residual = apply_gate(predicted - observed, gate_start, gate_stop)
         grad_local = adjoint(residual, left_bases, right_bases, rank_keep)
-        gradient = lax.psum(grad_local.astype(jnp.bfloat16), "row").astype(jnp.float32)
+        gradient = summed_here(grad_local.astype(jnp.bfloat16), "row").astype(jnp.float32)
         estimate = estimate - step_length * gradient
         low_model = estimate.astype(jnp.bfloat16)
     predicted = forward(low_model, left_bases, right_bases, rank_keep)

time: 338 us -> 270 us (0.80)
  the two profiles are of different devices: /device:TPU:6 before, /device:TPU:1 now
where the time goes in v1:
time: 270 us; the launch traced here: 265 us
  matrix products  82.3 us (30%)
  waiting for transfers between devices  70 us (26%)
  blocking collectives  57.9 us (21%)
  local copies, waits for them, and re-layouts  20.4 us (8%)
  between operations  15.2 us (6%)
  starting transfers between devices  13.1 us (5%)
  other arithmetic  5.85 us (2%)
    all_gather x2, waiting for transfers between devices, summed_here(): shards = lax.all_gather(shard, axis, axis=0, tiled=False)  44.7 us
    all_to_all x2, blocking collectives, forward(): lax.all_to_all(sendable, 'col', split_axis=0, concat_axis=1, tiled=True)  41.3 us
    dot_general x3, matrix products, forward(): jnp.einsum('jfavcs,ijfkcs->ijfavk', paired, right_bases, preferred_elemen...  27.3 us
    dot_general x3, matrix products, forward(): jnp.einsum('ijfavk,ijfkcn->ifavcn', received, left_bases, preferred_eleme...  20.6 us
    all_to_all x1, blocking collectives, adjoint(): lax.all_to_all(sendable, 'col', split_axis=1, concat_axis=0, tiled=True)  16.5 us
    dot_general x2, matrix products, adjoint(): jnp.einsum('ifavcn,ijfkcn->ijfavk', paired, left_bases, preferred_element...  15.2 us
    dot_general x2, matrix products, adjoint(): jnp.einsum('ijfavk,ijfkcs->jfavcs', received, right_bases, preferred_elem...  13.8 us
    all_to_all x1, waiting for transfers between devices, forward(): lax.all_to_all(sendable, 'col', split_axis=0, concat_axis=1, tiled=True)  13 us
  transfers between devices with their start and end apart: 4, of which 4 were waited for; matrix products, arithmetic and copies ran while one was open for 0% of the time, Pallas kernels for 0%

profile of v1, /device:TPU:1, one launch (start us, length us, event | category | flops | bytes accessed | tf_op | source)
XLA Modules:
  0.0 264.6 jit_solution(7006855825519075777)
XLA Ops:
  7.2 0.8 fusion.96
  8.0 1.0 convert_element_type.111
  9.1 9.1 %fusion.24 = bf16[16,4,2,2,16,96]{5,4,0,3,2,1:T(8,128)(2,1)S(1)} fusion(bf16[16,4,2,96,2,256,1]{5,4,3,2,1,0,6:T(2,128)(2,1)} %bitcast.378, f32[16,4,2,96]{3,0,2,1:T(8,128)S(1)} %get-tuple-element.31, bf16[2,1,16,4,2,256]{5,2,4,1,0,3:T(8,128)(2,1)S(1)} %get-tuple-element.19, bf16[2,1,16,4,2,256]{5,2,4,1,0,3:T(8,128)(2,1)S(1)} %get-tuple-element.18), kind=kOutput, calls=%fused_computation.33 | convolution fusion | flops 403963904 | bytes 13680640 | tf_op jit(solution)/shard_map/jfavcs,ijfkcs->ijfavk/dot_general | solution.py:61
  18.2 1.2 reshape.457
  19.4 1.7 copy.96
  21.1 9.1 %all-to-all-start = ((bf16[16,4,2,2,1536]{4,3,2,1,0:T(2,128)(2,1)}), bf16[16,4,2,2,1536]{4,3,2,1,0:T(2,128)(2,1)S(1)}, u32[]{:S(2)}, u32[]{:S(2)}) async-start(bf16[16,4,2,2,1536]{4,3,2,1,0:T(2,128)(2,1)} %copy.96), calls=%async_computation | async-start | bytes 1572864 | tf_op jit(solution)/shard_map/all_to_all | solution.py:66
  30.4 13.0 %all-to-all-done = bf16[16,4,2,2,1536]{4,3,2,1,0:T(2,128)(2,1)S(1)} async-done(((bf16[16,4,2,2,1536]{4,3,2,1,0:T(2,128)(2,1)}), bf16[16,4,2,2,1536]{4,3,2,1,0:T(2,128)(2,1)S(1)}, u32[]{:S(2)}, u32[]{:S(2)}) %all-to-all-start) | async-done | bytes 786464 | tf_op jit(solution)/shard_map/all_to_all | solution.py:66
  43.8 0.9 reshape.477
  44.7 6.9 %fusion.47 = f32[1,2,2,16,2,256]{5,3,4,2,1,0:T(8,128)S(1)} fusion(bf16[64,2,96,2,256,1]{4,3,2,1,0,5:T(2,128)(2,1)} %bitcast.349, bf16[64,2,2,16,96,1]{4,3,0,2,1,5:T(8,128)(2,1)S(1)} %reshape.477), kind=kOutput, calls=%fused_computation.40 | convolution fusion | flops 402653184 | bytes 13500416 | tf_op jit(solution)/shard_map/ijfavk,ijfkcn->ifavcn/dot_general | solution.py:68
  51.7 1.2 convolution_select_fusion.2
  52.9 0.6 fusion.20
  53.6 7.6 %fusion.35 = bf16[1,64,2,2,16,96]{5,4,1,3,2,0:T(8,128)(2,1)S(1)} fusion(bf16[64,2,96,2,256,1]{4,3,2,1,0,5:T(2,128)(2,1)} %bitcast.350, bf16[2,1,16,1,2,256]{5,2,4,1,0,3:T(8,128)(2,1)S(1)} %get-tuple-element.29, bf16[2,1,16,1,2,256]{5,2,4,1,0,3:T(8,128)(2,1)S(1)} %get-tuple-element.28), kind=kOutput, calls=%fused_computation.36 | convolution fusion | flops 403177472 | bytes 13434880 | tf_op jit(solution)/shard_map/ifavcn,ijfkcn->ijfavk/dot_general | solution.py:77
  61.2 1.2 reshape.462
  62.4 1.7 copy.106
  64.1 3.7 %all-to-all-start.1 = ((bf16[1,64,2,2,1536]{4,3,2,0,1:T(2,128)(2,1)}), bf16[1,64,2,2,1536]{4,3,2,0,1:T(2,128)(2,1)S(1)}, u32[]{:S(2)}, u32[]{:S(2)}) async-start(bf16[1,64,2,2,1536]{4,3,2,0,1:T(2,128)(2,1)} %copy.106), calls=%async_computation.1 | async-start | bytes 1572864 | tf_op jit(solution)/shard_map/all_to_all | solution.py:82
  68.1 12.2 %all-to-all-done.1 = bf16[1,64,2,2,1536]{4,3,2,0,1:T(2,128)(2,1)S(1)} async-done(((bf16[1,64,2,2,1536]{4,3,2,0,1:T(2,128)(2,1)}), bf16[1,64,2,2,1536]{4,3,2,0,1:T(2,128)(2,1)S(1)}, u32[]{:S(2)}, u32[]{:S(2)}) %all-to-all-start.1) | async-done | bytes 786464 | tf_op jit(solution)/shard_map/all_to_all | solution.py:82
  80.4 0.9 reshape.463
  81.2 6.9 %fusion.41 = f32[4,2,2,16,2,256]{5,3,4,2,1,0:T(8,128)S(1)} fusion(bf16[16,4,2,96,2,256,1]{5,4,3,2,1,0,6:T(2,128)(2,1)} %bitcast.379, bf16[16,4,2,2,16,96]{5,4,1,0,3,2:T(8,128)(2,1)S(1)} %reshape.463, bf16[16,4,2,96]{3,1,0,2:T(4,128)(2,1)S(1)} %copy.108), kind=kOutput, calls=%fused_computation.38 | convolution fusion | flops 403046400 | bytes 13918208 | tf_op jit(solution)/shard_map/ijfavk,ijfkcs->jfavcs/dot_general | solution.py:85
  88.3 0.7 convert_element_type.121
  89.1 23.6 %all-gather.3.cloned.1.call-done = bf16[8,2,2,16,1024]{4,3,2,1,0:T(8,128)(2,1)} async-done(((bf16[1,2,2,16,1024]{4,3,2,1,0:T(8,128)(2,1)}), bf16[8,2,2,16,1024]{4,3,2,1,0:T(8,128)(2,1)}) %all-gather.3.cloned.1.call-update) | async-done | bytes 1048592 | tf_op jit(solution)/shard_map/all_gather | solution.py:17
  112.7 1.4 reduce_sum.24
  114.3 9.1 %fusion.23 = bf16[16,4,2,2,16,96]{5,4,0,3,2,1:T(8,128)(2,1)S(1)} fusion(bf16[16,4,2,96,2,256,1]{5,4,3,2,1,0,6:T(2,128)(2,1)} %bitcast.380, f32[16,4,2,96]{3,0,2,1:T(8,128)S(1)} %get-tuple-element.31, bf16[2,1,16,4,2,256]{5,2,4,1,0,3:T(8,128)(2,1)S(1)} %get-tuple-element.15, bf16[2,1,16,4,2,256]{5,2,4,1,0,3:T(8,128)(2,1)S(1)} %get-tuple-element.14), kind=kOutput, calls=%fused_computation.31 | convolution fusion | flops 403963904 | bytes 13680640 | tf_op jit(solution)/shard_map/jfavcs,ijfkcs->ijfavk/dot_general | solution.py:61
  123.4 1.2 reshape.464
  124.6 0.8 copy.119
  125.5 20.6 %all_to_all.20 = bf16[16,4,2,2,1536]{4,3,2,1,0:T(2,128)(2,1)S(1)} all-to-all(bf16[16,4,2,2,1536]{4,3,2,1,0:T(2,128)(2,1)S(1)} %copy.119), channel_id=1, replica_groups=mesh['row'=8,'col'=16] {'col'}, dimensions={0} | all-to-all | bytes 1572864 | tf_op jit(solution)/shard_map/all_to_all | solution.py:66
  146.4 0.9 reshape.489
  147.3 6.9 %fusion.50 = f32[1,2,2,16,2,256]{5,3,4,2,1,0:T(8,128)S(1)} fusion(bf16[64,2,96,2,256,1]{4,3,2,1,0,5:T(2,128)(2,1)} %bitcast.351, bf16[64,2,2,16,96,1]{4,3,0,2,1,5:T(8,128)(2,1)S(1)} %reshape.489), kind=kOutput, calls=%fused_computation.41 | convolution fusion | flops 402653184 | bytes 13500416 | tf_op jit(solution)/shard_map/ijfavk,ijfkcn->ifavcn/dot_general | solution.py:68
  154.3 1.2 convolution_select_fusion.1
  155.5 0.6 fusion.21
  156.2 7.6 %fusion.38 = bf16[1,64,2,2,16,96]{5,4,1,3,2,0:T(8,128)(2,1)S(1)} fusion(bf16[64,2,96,2,256,1]{4,3,2,1,0,5:T(2,128)(2,1)} %bitcast.352, bf16[2,1,16,1,2,256]{5,2,4,1,0,3:T(8,128)(2,1)S(1)} %get-tuple-element.27, bf16[2,1,16,1,2,256]{5,2,4,1,0,3:T(8,128)(2,1)S(1)} %get-tuple-element.26), kind=kOutput, calls=%fused_computation.37 | convolution fusion | flops 403177472 | bytes 13434880 | tf_op jit(solution)/shard_map/ifavcn,ijfkcn->ijfavk/dot_general | solution.py:77
  163.8 1.2 reshape.468
  165.1 0.8 copy.129
  165.9 16.5 %all_to_all.21 = bf16[1,64,2,2,1536]{4,3,2,0,1:T(2,128)(2,1)S(1)} all-to-all(bf16[1,64,2,2,1536]{4,3,2,0,1:T(2,128)(2,1)S(1)} %copy.129), channel_id=1, replica_groups=mesh['row'=8,'col'=16] {'col'}, dimensions={1} | all-to-all | bytes 1572864 | tf_op jit(solution)/shard_map/all_to_all | solution.py:82
  182.5 0.9 reshape.469
  183.4 6.9 %fusion.44 = f32[4,2,2,16,2,256]{5,3,4,2,1,0:T(8,128)S(1)} fusion(bf16[16,4,2,96,2,256,1]{5,4,3,2,1,0,6:T(2,128)(2,1)} %bitcast.381, bf16[16,4,2,2,16,96]{5,4,1,0,3,2:T(8,128)(2,1)S(1)} %reshape.469, bf16[16,4,2,96]{3,1,0,2:T(4,128)(2,1)S(1)} %copy.108), kind=kOutput, calls=%fused_computation.39 | convolution fusion | flops 403046400 | bytes 13918208 | tf_op jit(solution)/shard_map/ijfavk,ijfkcs->jfavcs/dot_general | solution.py:85
  190.5 0.7 convert_element_type.131
  191.2 21.2 %all-gather.5.cloned.1.call-done = bf16[8,2,2,16,1024]{4,3,2,1,0:T(8,128)(2,1)} async-done(((bf16[1,2,2,16,1024]{4,3,2,1,0:T(8,128)(2,1)}), bf16[8,2,2,16,1024]{4,3,2,1,0:T(8,128)(2,1)}) %all-gather.5.cloned.1.call-update) | async-done | bytes 1048592 | tf_op jit(solution)/shard_map/all_gather | solution.py:17
  212.4 1.4 reduce_sum.25
  213.8 0.8 fusion.105
  214.8 9.1 %fusion.22 = bf16[16,4,2,2,16,96]{5,4,0,3,2,1:T(8,128)(2,1)S(1)} fusion(bf16[16,4,2,96,2,256,1]{5,4,3,2,1,0,6:T(2,128)(2,1)} %bitcast.382, f32[16,4,2,96]{3,0,2,1:T(8,128)S(1)} %get-tuple-element.31, bf16[2,1,16,4,2,256]{5,2,4,1,0,3:T(8,128)(2,1)S(1)} %get-tuple-element.11, bf16[2,1,16,4,2,256]{5,2,4,1,0,3:T(8,128)(2,1)S(1)} %get-tuple-element.10), kind=kOutput, calls=%fused_computation.29 | convolution fusion | flops 403963904 | bytes 13680640 | tf_op jit(solution)/shard_map/jfavcs,ijfkcs->ijfavk/dot_general | solution.py:61
  223.9 1.2 reshape.470
  225.1 0.8 copy.141
  225.9 20.7 %all_to_all.22 = bf16[16,4,2,2,1536]{4,3,2,1,0:T(2,128)(2,1)S(1)} all-to-all(bf16[16,4,2,2,1536]{4,3,2,1,0:T(2,128)(2,1)S(1)} %copy.141), channel_id=1, replica_groups=mesh['row'=8,'col'=16] {'col'}, dimensions={0} | all-to-all | bytes 1572864 | tf_op jit(solution)/shard_map/all_to_all | solution.py:66
  246.9 0.9 reshape.501
  247.8 6.9 %fusion.53 = f32[1,2,2,16,2,256]{5,3,4,2,1,0:T(8,128)S(1)} fusion(bf16[64,2,96,2,256,1]{4,3,2,1,0,5:T(2,128)(2,1)} %bitcast.353, bf16[64,2,2,16,96,1]{4,3,0,2,1,5:T(8,128)(2,1)S(1)} %reshape.501), kind=kOutput, calls=%fused_computation.42 | convolution fusion | flops 402653184 | bytes 13500416 | tf_op jit(solution)/shard_map/ijfavk,ijfkcn->ifavcn/dot_general | solution.py:68
  254.8 1.2 convolution_select_fusion
  256.0 0.6 convolution_multiply_fusion
  256.6 0.6 copy.219
  (71 shorter events, 2.7 us)
Async XLA Ops:
  7.2 23.1 %copy-start.2 = (s32[16,256]{1,0:T(8,128)S(1)}, s32[16,256]{1,0:T(8,128)}, u32[]{:S(2)}) copy-start(s32[16,256]{1,0:T(8,128)} %param.12) | copy-start | bytes 49156
  7.2 23.1 %copy-start.3 = (s32[16,256]{1,0:T(8,128)S(1)}, s32[16,256]{1,0:T(8,128)}, u32[]{:S(2)}) copy-start(s32[16,256]{1,0:T(8,128)} %param.13) | copy-start | bytes 49156
  18.2 33.4 %copy-start.1 = (f32[2,2,16,256]{3,2,1,0:T(8,128)S(1)}, f32[2,2,16,256]{3,2,1,0:T(8,128)}, u32[]{:S(2)}) copy-start(f32[2,2,16,256]{3,2,1,0:T(8,128)} %param.8) | copy-start | bytes 196612
  21.1 22.3 %all-to-all-start = ((bf16[16,4,2,2,1536]{4,3,2,1,0:T(2,128)(2,1)}), bf16[16,4,2,2,1536]{4,3,2,1,0:T(2,128)(2,1)S(1)}, u32[]{:S(2)}, u32[]{:S(2)}) async-start(bf16[16,4,2,2,1536]{4,3,2,1,0:T(2,128)(2,1)} %copy.96), calls=%async_computation | async-start | bytes 1572864 | tf_op jit(solution)/shard_map/all_to_all | solution.py:66
  62.4 51.7 %copy-start = (f32[2,2,16,1024]{3,2,1,0:T(8,128)S(1)}, f32[2,2,16,1024]{3,2,1,0:T(8,128)}, u32[]{:S(2)}) copy-start(f32[2,2,16,1024]{3,2,1,0:T(8,128)} %param.7) | copy-start | bytes 786436
  64.1 16.1 %all-to-all-start.1 = ((bf16[1,64,2,2,1536]{4,3,2,0,1:T(2,128)(2,1)}), bf16[1,64,2,2,1536]{4,3,2,0,1:T(2,128)(2,1)S(1)}, u32[]{:S(2)}, u32[]{:S(2)}) async-start(bf16[1,64,2,2,1536]{4,3,2,0,1:T(2,128)(2,1)} %copy.106), calls=%async_computation.1 | async-start | bytes 1572864 | tf_op jit(solution)/shard_map/all_to_all | solution.py:82
  67.8 44.9 %all-gather.3.cloned.1.call-start = ((), (), s32[]{:S(2)}) async-start(), calls=%async_computation.5 | async-start | bytes 1179648 | tf_op jit(solution)/shard_map/all_gather | solution.py:17
  89.1 123.3 %all-gather.5.cloned.1.call-start = ((), (), s32[]{:S(2)}) async-start(), calls=%async_computation.6 | async-start | bytes 1179648 | tf_op jit(solution)/shard_map/all_gather | solution.py:17
Sparse Core Ops, SparseCore 0:
  89.2 23.4 all-gather.2
  191.3 21.0 all-gather.4
